TPU v7x, 32 devices: a whole 2x2x4 slice. The times are simulated.
32 devices in a mesh: group: 4 (over y, x), dp: 2 (over core), tensor: 4 (over z).
Axes of the slice: x: 2, y: 2, z: 4, core: 2. Of those that a mesh axis runs over, the one named last changes fastest.
Arguments:
- tokens: bfloat16 [8192, 2048], P(('group', 'dp')), may hold values from -6 to 6
- norm_gain: bfloat16 [2048], replicated, may hold values from 0.099609375 to 1.8984375
- w_query: bfloat16 [2048, 2048], P(None, 'tensor'), may hold values from -0.25 to 0.25
- w_keyval: bfloat16 [2048, 512], P(None, 'tensor'), may hold values from -0.125 to 0.125
- w_out: bfloat16 [2048, 2048], P('tensor'), may hold values from -0.8984375 to 0.8984375
- kv_cache: bfloat16 [4, 32, 16, 128, 512], P(None, ('group', 'dp'), None, None, 'tensor'), may hold values from -400 to 400
- lengths: int32 [32, 2], P(('group', 'dp')), may hold values from 0 to 2048, as said below
- dest_slot: int32 [32, 16], replicated, may hold values from 0 to 511, as said below
Outputs:
- mixed: bfloat16 [8192, 2048], P(('group', 'dp', 'tensor'))
- decode_cache: bfloat16 [4, 512, 128, 512], P(None, ('group', 'dp'), None, 'tensor')
Inputs may be any that keep to these rules, and one draw needn't show every extreme that they name: lengths[p, 0] lies in 0 to 2048 and lengths[p, 1] in 1 to 256; 2048 and 256 are each taken by some prompt; the prompts r * 4 to r * 4 + 3 of each index r of group and dp together hold exactly 32 live blocks. dest_slot is a permutation of the 512 slots; the slots of the index r of group and dp together are r * 4 * 16 onward; the blocks of prompts r * 4 to r * 4 + 3 send exactly 8 blocks to each index, of which exactly 4 is live.
All inputs are finite; a program needn't handle non-finite values.
Results may differ from a plain program's by a relative error of at most 0.009.
Values may be sent and summed in bfloat16 or wider, within the bound.
A program may use at most 128 MiB of HBM per device.

v0:
```python
import jax
import jax.numpy as jnp
from jax import lax
from jax.sharding import PartitionSpec as P

HD = 64


def per_device(tokens, norm_gain, w_query, w_keyval, w_out, kv_cache, lengths, dest_slot):
    tok_rows = tokens.shape[0]
    prompts = lengths.shape[0]
    fresh_rows = tok_rows // prompts
    heads_local = w_query.shape[1] // HD
    kv_local = w_keyval.shape[1] // (2 * HD)
    group_size = heads_local // kv_local
    layers = kv_cache.shape[0]
    blocks_win = kv_cache.shape[2]
    block_len = kv_cache.shape[3]
    lane_width = kv_cache.shape[4]
    window = blocks_win * block_len
    tokens_f = tokens.astype(jnp.float32)
    normed = (
        tokens_f
        * lax.rsqrt(jnp.mean(tokens_f * tokens_f, axis=-1, keepdims=True) + 1e-05)
        * norm_gain.astype(jnp.float32)
    ).astype(jnp.bfloat16)
    query = jnp.dot(normed, w_query, preferred_element_type=jnp.float32).astype(jnp.bfloat16)
    query = query.reshape(prompts, fresh_rows, kv_local, group_size, HD)
    keyval = jnp.dot(normed, w_keyval, preferred_element_type=jnp.float32).astype(jnp.bfloat16)
    keyval = keyval.reshape(prompts, fresh_rows, kv_local, 2, HD)
    cache = kv_cache[0].reshape(prompts, window, kv_local, 2, HD)
    scale = 1.0 / HD**0.5
    query_pos = jnp.arange(fresh_rows)[:, None]
    key_pos = jnp.arange(window + fresh_rows)[None, :]

    def attend(items):
        query_p, cache_p, fresh_p, history, fresh_len = items
        pairs = jnp.concatenate([cache_p, fresh_p], axis=0)
        scores = (
            jnp.einsum(
                "ckgd,tkd->kgct", query_p, pairs[:, :, 0], preferred_element_type=jnp.float32
            )
            * scale
        )
        visible = jnp.where(
            key_pos < window,
            (key_pos >= window - history) & (key_pos >= query_pos + 1),
            key_pos - window <= query_pos,
        )
        scores = jnp.where(visible, scores, -1e30)
        scores = scores - jnp.max(scores, axis=-1, keepdims=True)
        expo = jnp.exp(scores)
        weights = (expo / jnp.sum(expo, axis=-1, keepdims=True)).astype(jnp.bfloat16)
        mixed_p = jnp.einsum(
            "kgct,tkd->ckgd", weights, pairs[:, :, 1], preferred_element_type=jnp.float32
        )
        mixed_p = mixed_p.astype(jnp.bfloat16).reshape(fresh_rows, heads_local * HD)
        return jnp.where(
            (jnp.arange(fresh_rows) < fresh_len)[:, None], mixed_p, jnp.zeros_like(mixed_p)
        )

    attn = lax.map(attend, (query, cache, keyval, lengths[:, 0], lengths[:, 1]))
    attn = attn.reshape(tok_rows, heads_local * HD)
    mixed = lax.psum_scatter(
        jnp.dot(attn, w_out, preferred_element_type=jnp.float32),
        "tensor",
        scatter_dimension=0,
        tiled=True,
    ).astype(jnp.bfloat16)
    per_dev = prompts * blocks_win
    devices = lax.axis_size(("group", "dp"))
    per_peer = per_dev // devices
    my_index = lax.axis_index(("group", "dp"))
    dest_all = dest_slot.reshape(devices, per_dev)
    recv_all = dest_all // per_dev
    same_dest = recv_all[:, :, None] == recv_all[:, None, :]
    earlier = jnp.arange(per_dev)[None, :] < jnp.arange(per_dev)[:, None]
    own_recv = lax.dynamic_index_in_dim(recv_all, my_index, 0, keepdims=False)
    senders = jnp.arange(devices, dtype=jnp.int32)[:, None]
    capacity = per_peer // 2
    lengths_every = lax.all_gather(lengths, ("group", "dp"), axis=0, tiled=True)
    live_all = (
        (jnp.arange(blocks_win)[None, :] + 1) * block_len > window - lengths_every[:, 0:1]
    ).reshape(devices, per_dev)
    live_rank = jnp.sum(same_dest & earlier[None, :, :] & live_all[:, None, :], axis=2)
    own_live = lax.dynamic_index_in_dim(live_all, my_index, 0, keepdims=False)
    own_live_rank = lax.dynamic_index_in_dim(live_rank, my_index, 0, keepdims=False)
    send_pos = jnp.where(own_live, own_recv * capacity + own_live_rank, devices * capacity)
    send_idx = (
        jnp.zeros((devices * capacity,), jnp.int32)
        .at[send_pos]
        .set(jnp.arange(per_dev, dtype=jnp.int32), mode="drop")
    )
    raw_blocks = kv_cache.reshape(layers, per_dev, block_len, lane_width)
    outgoing = jnp.take(raw_blocks, send_idx, axis=1)
    incoming = lax.all_to_all(outgoing, ("group", "dp"), split_axis=1, concat_axis=1, tiled=True)
    where_from = senders * capacity + live_rank
    valid = (recv_all == my_index) & live_all
    slot_local = jnp.where(valid, dest_all - my_index * per_dev, per_dev)
    source_idx = (
        jnp.full((per_dev,), devices * capacity, jnp.int32)
        .at[slot_local.reshape(-1)]
        .set(where_from.reshape(-1), mode="drop")
    )
    decode_cache = jnp.take(incoming, source_idx, axis=1, mode="fill", fill_value=0)
    return (mixed, decode_cache)


def solution(mesh):
    in_specs = (
        P(("group", "dp"), None),
        P(),
        P(None, "tensor"),
        P(None, "tensor"),
        P("tensor", None),
        P(None, ("group", "dp"), None, None, "tensor"),
        P(("group", "dp"), None),
        P(),
    )
    out_specs = (P(("group", "dp", "tensor"), None), P(None, ("group", "dp"), None, "tensor"))
    return jax.shard_map(
        per_device, mesh=mesh, in_specs=in_specs, out_specs=out_specs, check_vma=False
    )
```

profile of v0, /device:TPU:0, one launch (start us, length us, event | category | flops | bytes accessed | tf_op | source)
XLA Modules:
  0.0 344.5 jit_solution(16174500329635103676)
XLA Ops:
  27.7 5.3 %convolution_convert_fusion = bf16[1024,512]{1,0:T(8,128)(2,1)S(1)} fusion(bf16[2048,512]{1,0:T(8,128)(2,1)} %param.12, bf16[1024,2048]{1,0:T(8,128)(2,1)} %param.10, f32[2048]{0:T(1024)S(1)} %convert_element_type.40, f32[1024]{0:T(1024)S(1)} %add_rsqrt_fusion), kind=kOutput, calls=%fused_computation.49 | convolution fusion | flops 2156396544 | bytes 7352320 | tf_op jit(solution)/shard_map/dot_general | solution.py:27
  38.1 142.6 %while.14 = (s32[]{:T(128)}, bf16[4,256,512]{2,1,0:T(8,128)(2,1)}, s32[4]{0:T(128)}, bf16[4,2048,1,2,64]{1,4,3,2,0:T(8,128)(2,1)}, bf16[4,256,1,2,64]{1,4,3,2,0:...) while((s32[]{:T(128)}, bf16[4,256,512]{2,1,0:T(8,128)(2,1)}, ...), condition=%wide.region_4.5_spmd.clone.clone, body=%wide.region_1.4_spmd.clone.clone.sunk | while | flops 1268387072 | bytes 63510268 | solution.py:62
  43.3 9.0 %fusion.59 = (f32[8,256]{1,0:T(8,128)S(1)}, f32[2304,256,8]{1,0,2:T(8,128)}) fusion(pred[256,2304]{0,1:T(8,128)(4,1)S(1)} %fusion.58, bf16[4,256,1,8,64]{1,4,3,2,0:T(8,128)(2,1)} %get-tuple-element.310, s32[]{:T(128)S(6)} %copy.74, bf16[256,1,2,64]{0,3,2,1:T(8,128)(2,1)S(1)} %dynamic-slice_bitcast_fusion.4, ...), kind=kOutput, calls=%fused_computation.10.clone.1 | convolution fusion | flops 618723328 | bytes 20324356 | tf_op jit(solution)/shard_map/while/body/eval_jaxpr/ckgd,tkd->kgct/dot_general | solution.py:40
  52.3 10.2 %fusion.60 = f32[8,256]{1,0:T(8,128)S(1)} fusion(f32[2304,256,8]{1,0,2:T(8,128)} %get-tuple-element.284, f32[8,256]{1,0:T(8,128)S(1)} %get-tuple-element.285, pred[256,2304]{0,1:T(8,128)(4,1)S(1)} %fusion.58), kind=kLoop, calls=%fused_computation.9.clone.1 | loop fusion | flops 18872320 | bytes 19480576 | tf_op jit(solution)/shard_map/while/body/eval_jaxpr/reduce_sum | solution.py:53
  62.5 9.0 %fusion.61 = bf16[64,8,256]{2,0,1:T(8,128)(2,1)S(1)} fusion(f32[8,256]{1,0:T(8,128)S(1)} %fusion.60, f32[8,256]{1,0:T(8,128)S(1)} %get-tuple-element.285, f32[2304,256,8]{1,0,2:T(8,128)} %get-tuple-element.284, pred[256,2304]{0,1:T(8,128)(4,1)S(1)} %fusion.58, bf16[2048,1,2,64]{0,3,2,1:T(8,128)(2,1)S(1)} %dynamic-slice_bitcast_fusion.5, ...), kind=kOutput, calls=%fused_computation.17.clone.1 | convolution fusion | flops 628293632 | bytes 20332544 | tf_op jit(solution)/shard_map/while/body/eval_jaxpr/kgct,tkd->ckgd/dot_general | solution.py:54
  78.9 9.0 %fusion.59 = (f32[8,256]{1,0:T(8,128)S(1)}, f32[2304,256,8]{1,0,2:T(8,128)}) fusion(pred[256,2304]{0,1:T(8,128)(4,1)S(1)} %fusion.58, bf16[4,256,1,8,64]{1,4,3,2,0:T(8,128)(2,1)} %get-tuple-element.310, s32[]{:T(128)S(6)} %copy.74, bf16[256,1,2,64]{0,3,2,1:T(8,128)(2,1)S(1)} %dynamic-slice_bitcast_fusion.4, ...), kind=kOutput, calls=%fused_computation.10.clone.1 | convolution fusion | flops 618723328 | bytes 20324356 | tf_op jit(solution)/shard_map/while/body/eval_jaxpr/ckgd,tkd->kgct/dot_general | solution.py:40
  87.9 10.2 %fusion.60 = f32[8,256]{1,0:T(8,128)S(1)} fusion(f32[2304,256,8]{1,0,2:T(8,128)} %get-tuple-element.284, f32[8,256]{1,0:T(8,128)S(1)} %get-tuple-element.285, pred[256,2304]{0,1:T(8,128)(4,1)S(1)} %fusion.58), kind=kLoop, calls=%fused_computation.9.clone.1 | loop fusion | flops 18872320 | bytes 19480576 | tf_op jit(solution)/shard_map/while/body/eval_jaxpr/reduce_sum | solution.py:53
  98.1 9.0 %fusion.61 = bf16[64,8,256]{2,0,1:T(8,128)(2,1)S(1)} fusion(f32[8,256]{1,0:T(8,128)S(1)} %fusion.60, f32[8,256]{1,0:T(8,128)S(1)} %get-tuple-element.285, f32[2304,256,8]{1,0,2:T(8,128)} %get-tuple-element.284, pred[256,2304]{0,1:T(8,128)(4,1)S(1)} %fusion.58, bf16[2048,1,2,64]{0,3,2,1:T(8,128)(2,1)S(1)} %dynamic-slice_bitcast_fusion.5, ...), kind=kOutput, calls=%fused_computation.17.clone.1 | convolution fusion | flops 628293632 | bytes 20332544 | tf_op jit(solution)/shard_map/while/body/eval_jaxpr/kgct,tkd->ckgd/dot_general | solution.py:54
  114.6 9.0 %fusion.59 = (f32[8,256]{1,0:T(8,128)S(1)}, f32[2304,256,8]{1,0,2:T(8,128)}) fusion(pred[256,2304]{0,1:T(8,128)(4,1)S(1)} %fusion.58, bf16[4,256,1,8,64]{1,4,3,2,0:T(8,128)(2,1)} %get-tuple-element.310, s32[]{:T(128)S(6)} %copy.74, bf16[256,1,2,64]{0,3,2,1:T(8,128)(2,1)S(1)} %dynamic-slice_bitcast_fusion.4, ...), kind=kOutput, calls=%fused_computation.10.clone.1 | convolution fusion | flops 618723328 | bytes 20324356 | tf_op jit(solution)/shard_map/while/body/eval_jaxpr/ckgd,tkd->kgct/dot_general | solution.py:40
  123.6 10.2 %fusion.60 = f32[8,256]{1,0:T(8,128)S(1)} fusion(f32[2304,256,8]{1,0,2:T(8,128)} %get-tuple-element.284, f32[8,256]{1,0:T(8,128)S(1)} %get-tuple-element.285, pred[256,2304]{0,1:T(8,128)(4,1)S(1)} %fusion.58), kind=kLoop, calls=%fused_computation.9.clone.1 | loop fusion | flops 18872320 | bytes 19480576 | tf_op jit(solution)/shard_map/while/body/eval_jaxpr/reduce_sum | solution.py:53
  133.8 9.0 %fusion.61 = bf16[64,8,256]{2,0,1:T(8,128)(2,1)S(1)} fusion(f32[8,256]{1,0:T(8,128)S(1)} %fusion.60, f32[8,256]{1,0:T(8,128)S(1)} %get-tuple-element.285, f32[2304,256,8]{1,0,2:T(8,128)} %get-tuple-element.284, pred[256,2304]{0,1:T(8,128)(4,1)S(1)} %fusion.58, bf16[2048,1,2,64]{0,3,2,1:T(8,128)(2,1)S(1)} %dynamic-slice_bitcast_fusion.5, ...), kind=kOutput, calls=%fused_computation.17.clone.1 | convolution fusion | flops 628293632 | bytes 20332544 | tf_op jit(solution)/shard_map/while/body/eval_jaxpr/kgct,tkd->ckgd/dot_general | solution.py:54
  150.2 9.0 %fusion.59 = (f32[8,256]{1,0:T(8,128)S(1)}, f32[2304,256,8]{1,0,2:T(8,128)}) fusion(pred[256,2304]{0,1:T(8,128)(4,1)S(1)} %fusion.58, bf16[4,256,1,8,64]{1,4,3,2,0:T(8,128)(2,1)} %get-tuple-element.310, s32[]{:T(128)S(6)} %copy.74, bf16[256,1,2,64]{0,3,2,1:T(8,128)(2,1)S(1)} %dynamic-slice_bitcast_fusion.4, ...), kind=kOutput, calls=%fused_computation.10.clone.1 | convolution fusion | flops 618723328 | bytes 20324356 | tf_op jit(solution)/shard_map/while/body/eval_jaxpr/ckgd,tkd->kgct/dot_general | solution.py:40
  159.2 10.2 %fusion.60 = f32[8,256]{1,0:T(8,128)S(1)} fusion(f32[2304,256,8]{1,0,2:T(8,128)} %get-tuple-element.284, f32[8,256]{1,0:T(8,128)S(1)} %get-tuple-element.285, pred[256,2304]{0,1:T(8,128)(4,1)S(1)} %fusion.58), kind=kLoop, calls=%fused_computation.9.clone.1 | loop fusion | flops 18872320 | bytes 19480576 | tf_op jit(solution)/shard_map/while/body/eval_jaxpr/reduce_sum | solution.py:53
  169.4 9.0 %fusion.61 = bf16[64,8,256]{2,0,1:T(8,128)(2,1)S(1)} fusion(f32[8,256]{1,0:T(8,128)S(1)} %fusion.60, f32[8,256]{1,0:T(8,128)S(1)} %get-tuple-element.285, f32[2304,256,8]{1,0,2:T(8,128)} %get-tuple-element.284, pred[256,2304]{0,1:T(8,128)(4,1)S(1)} %fusion.58, bf16[2048,1,2,64]{0,3,2,1:T(8,128)(2,1)S(1)} %dynamic-slice_bitcast_fusion.5, ...), kind=kOutput, calls=%fused_computation.17.clone.1 | convolution fusion | flops 628293632 | bytes 20332544 | tf_op jit(solution)/shard_map/while/body/eval_jaxpr/kgct,tkd->ckgd/dot_general | solution.py:54
  180.8 6.8 %fusion.45 = f32[1024,2048]{1,0:T(8,128)} fusion(bf16[1024,512]{1,0:T(8,128)(2,1)} %bitcast.102, bf16[512,2048]{1,0:T(8,128)(2,1)S(1)} %copy-done), kind=kOutput, calls=%fused_computation.92 | convolution fusion | flops 2147483648 | bytes 11534336 | tf_op jit(solution)/shard_map/dot_general | solution.py:65
  187.8 10.3 %all-gather = s32[8,4,2]{1,2,0:T(2,128)S(1)} all-gather(s32[1,4,2]{1,2,0:T(2,128)S(1)} %bitcast.100), channel_id=1, replica_groups=mesh['group'=4,'dp'=2,'tensor'=4] {'group','dp'}, dimensions={0}, use_global_device_ids=true | all-gather | bytes 288 | tf_op jit(solution)/shard_map/all_gather | solution.py:81
  200.0 6.5 %gather_fusion = bf16[32,4,128,128]{3,2,1,0:T(8,128)(2,1)} fusion(bf16[4,64,128,128]{3,2,1,0:T(8,128)(2,1)} %bitcast.99, s32[1024]{0:T(1024)S(1)} %pad_clamp_fusion.1), kind=kCustom, calls=%fused_computation | custom fusion | bytes 8388736 | tf_op jit(solution)/shard_map/jit(_take)/gather | solution.py:95
  206.5 4.7 %select_bitcast_fusion.1 = bf16[4,32,128,128]{3,2,0,1:T(8,128)(2,1)} fusion(bf16[32,4,128,128]{3,2,1,0:T(8,128)(2,1)} %gather_fusion, pred[32]{0:T(512)(128)(4,1)S(1)} %compare_and_fusion), kind=kLoop, calls=%fused_computation.48 | loop fusion | flops 2097152 | bytes 8388640 | tf_op jit(solution)/shard_map/jit(_take)/select_n | solution.py:95
  218.7 46.2 %all-to-all-done = bf16[4,32,128,128]{3,2,0,1:T(8,128)(2,1)} async-done(((bf16[4,32,128,128]{3,2,0,1:T(8,128)(2,1)}), bf16[4,32,128,128]{3,2,0,1:T(8,128)(2,1)}, u32[]{:S(2)}, u32[]{:S(2)}) %all-to-all-start) | async-done | bytes 4194336 | tf_op jit(solution)/shard_map/all_to_all | solution.py:96
  264.9 4.7 %copy.60 = bf16[4,32,128,128]{3,2,1,0:T(8,128)(2,1)} copy(bf16[4,32,128,128]{3,2,0,1:T(8,128)(2,1)} %all-to-all-done) | data formatting | bytes 8388608 | tf_op jit(solution)/shard_map/all_to_all | solution.py:96
  269.6 7.8 %gather_fusion.1 = bf16[64,4,128,128]{3,2,1,0:T(8,128)(2,1)} fusion(bf16[4,32,128,128]{3,2,1,0:T(8,128)(2,1)} %copy.60, s32[1024]{0:T(1024)S(1)} %pad_clamp_fusion), kind=kCustom, calls=%fused_computation.1 | custom fusion | bytes 16777472 | tf_op jit(solution)/shard_map/jit(_take)/gather | solution.py:105
  277.4 7.3 %select_bitcast_fusion = bf16[4,64,128,128]{3,2,0,1:T(8,128)(2,1)} fusion(bf16[64,4,128,128]{3,2,1,0:T(8,128)(2,1)} %gather_fusion.1, pred[64]{0:T(512)(128)(4,1)S(1)} %compare_and_fusion.1), kind=kLoop, calls=%fused_computation.47 | loop fusion | flops 4194304 | bytes 16777280 | tf_op jit(solution)/shard_map/jit(_take)/select_n | solution.py:105
  284.7 10.5 %copy.61 = bf16[4,64,128,128]{3,2,1,0:T(8,128)(2,1)} copy(bf16[4,64,128,128]{3,2,0,1:T(8,128)(2,1)} %select_bitcast_fusion) | data formatting | bytes 16777216
  295.2 39.7 %reduce-scatter.2.cloned.1.call-done = f32[256,2048]{1,0:T(8,128)} async-done(((f32[1024,2048]{1,0:T(8,128)}), f32[256,2048]{1,0:T(8,128)}) %reduce-scatter.2.cloned.1.call-update) | async-done | bytes 2097168 | tf_op jit(solution)/shard_map/reduce_scatter | solution.py:64
  (114 shorter events, 64.6 us)
Async XLA Ops:
  7.2 173.6 %copy-start = (bf16[512,2048]{1,0:T(8,128)(2,1)S(1)}, bf16[512,2048]{1,0:T(8,128)(2,1)}, u32[]{:S(2)}) copy-start(bf16[512,2048]{1,0:T(8,128)(2,1)} %param.14) | copy-start | bytes 6291460
  7.2 13.2 %copy-start.2 = (bf16[2048]{0:T(1024)(128)(2,1)S(1)}, bf16[2048]{0:T(1024)(128)(2,1)}, u32[]{:S(2)}) copy-start(bf16[2048]{0:T(1024)(128)(2,1)} %param.11) | copy-start | bytes 12292
  7.2 327.7 %reduce-scatter.2.cloned.1.call-start = ((), (), s32[]{:S(2)}) async-start(), calls=%async_computation.2 | async-start | bytes 10485760 | tf_op jit(solution)/shard_map/reduce_scatter | solution.py:64
  62.4 9.1 %copy-start.4 = (s32[4]{0:T(128)S(1)}, s32[4]{0:T(128)}, u32[]{:S(2)}) copy-start(s32[4]{0:T(128)} %get-tuple-element.306) | copy-start | bytes 52 | tf_op jit(solution)/shard_map/while
  98.1 9.1 %copy-start.4 = (s32[4]{0:T(128)S(1)}, s32[4]{0:T(128)}, u32[]{:S(2)}) copy-start(s32[4]{0:T(128)} %get-tuple-element.306) | copy-start | bytes 52 | tf_op jit(solution)/shard_map/while
  133.8 9.1 %copy-start.4 = (s32[4]{0:T(128)S(1)}, s32[4]{0:T(128)}, u32[]{:S(2)}) copy-start(s32[4]{0:T(128)} %get-tuple-element.306) | copy-start | bytes 52 | tf_op jit(solution)/shard_map/while
  169.4 9.1 %copy-start.4 = (s32[4]{0:T(128)S(1)}, s32[4]{0:T(128)}, u32[]{:S(2)}) copy-start(s32[4]{0:T(128)} %get-tuple-element.306) | copy-start | bytes 52 | tf_op jit(solution)/shard_map/while
  180.8 6.8 %copy-start.1 = (s32[32,16]{0,1:T(8,128)S(1)}, s32[32,16]{0,1:T(8,128)}, u32[]{:S(2)}) copy-start(s32[32,16]{0,1:T(8,128)} %param.17) | copy-start | bytes 6148
  180.8 7.0 %copy-start.3 = (s32[4,2]{0,1:T(2,128)S(1)}, s32[4,2]{0,1:T(2,128)}, u32[]{:S(2)}) copy-start(s32[4,2]{0,1:T(2,128)} %param.16) | copy-start | bytes 100
  211.1 53.7 %all-to-all-start = ((bf16[4,32,128,128]{3,2,0,1:T(8,128)(2,1)}), bf16[4,32,128,128]{3,2,0,1:T(8,128)(2,1)}, u32[]{:S(2)}, u32[]{:S(2)}) async-start(bf16[4,32,128,128]{3,2,0,1:T(8,128)(2,1)} %select_bitcast_fusion.1), calls=%async_computation.1 | async-start | bytes 8388608 | tf_op jit(solution)/shard_map/all_to_all | solution.py:96
Sparse Core Ops, SparseCore 0:
  187.7 147.1 reduce-scatter.1
where the time goes:
time: 346 us; the launch traced here: 344 us
  matrix products  87.7 us (25%)
  waiting for transfers between devices  85.9 us (25%)
  other arithmetic  70.1 us (20%)
  local copies, waits for them, and re-layouts  68.4 us (20%)
  between operations  14.2 us (4%)
  blocking collectives  10.3 us (3%)
  starting transfers between devices  4.64 us (1%)
    all_to_all x1, waiting for transfers between devices, per_device(): lax.all_to_all(outgoing, ('group', 'dp'), split_axis=1, concat_axis=1, ti...  46.2 us
    reduce_sum x4, other arithmetic, attend(): jnp.sum(expo, axis=-1, keepdims=True)  40.7 us
    reduce_scatter x1, waiting for transfers between devices, per_device(): lax.psum_scatter(jnp.dot(attn, w_out, preferred_element_type=jnp.float32)...  39.7 us
    dot_general x4, matrix products, attend(): jnp.einsum('kgct,tkd->ckgd', weights, pairs[:, :, 1], preferred_element_t...  36.2 us
    dot_general x4, matrix products, attend(): jnp.einsum('ckgd,tkd->kgct', query_p, pairs[:, :, 0], preferred_element_t...  35.9 us
    unnamed x13, local copies, waits for them, and re-layouts  14.1 us
    all_gather x1, blocking collectives, per_device(): lengths_every = lax.all_gather(lengths, ('group', 'dp'), axis=0, tiled=True)  10.3 us
    select_n x4, other arithmetic, attend(): jnp.where(key_pos < window, (key_pos >= window - history) & (key_pos >= q...  8.15 us
  transfers between devices with their start and end apart: 2, of which 2 were waited for; matrix products, arithmetic and copies ran while one was open for 13% of the time, Pallas kernels for 0%

commit v1 on v0

--- a/solution.py
+++ b/solution.py
@@ -78,7 +78,39 @@
     own_recv = lax.dynamic_index_in_dim(recv_all, my_index, 0, keepdims=False)
     senders = jnp.arange(devices, dtype=jnp.int32)[:, None]
     capacity = per_peer // 2
-    lengths_every = lax.all_gather(lengths, ("group", "dp"), axis=0, tiled=True)
+    v_now, plain, parts_out = (
+        lax.axis_size(("group", "dp")),
+        lax.axis_index(("group", "dp")),
+        lengths.shape[0],
+    )
+    lengths_every = lax.dynamic_update_slice_in_dim(
+        jnp.zeros(
+            [idx * v_now if src_i == 0 else idx for src_i, idx in enumerate(lengths.shape)],
+            lengths.dtype,
+        ),
+        lengths,
+        plain * parts_out,
+        axis=0,
+    )
+    mat_out = all_values = lengths
+    for hop_no in range(1, v_now // 2 + 1):
+        mat_out = lax.ppermute(
+            mat_out,
+            axis_name=("group", "dp"),
+            perm=[(src_i, (src_i + 1) % v_now) for src_i in range(v_now)],
+        )
+        lengths_every = lax.dynamic_update_slice_in_dim(
+            lengths_every, mat_out, (plain - hop_no) % v_now * parts_out, axis=0
+        )
+        if 2 * hop_no < v_now:
+            all_values = lax.ppermute(
+                all_values,
+                axis_name=("group", "dp"),
+                perm=[(src_i, (src_i - 1) % v_now) for src_i in range(v_now)],
+            )
+            lengths_every = lax.dynamic_update_slice_in_dim(
+                lengths_every, all_values, (plain + hop_no) % v_now * parts_out, axis=0
+            )
     live_all = (
         (jnp.arange(blocks_win)[None, :] + 1) * block_len > window - lengths_every[:, 0:1]
     ).reshape(devices, per_dev)

time: 346 us -> 346 us (level)
  blocking collectives: 10.3 us -> 0 us
  starting transfers between devices: 4.64 us -> 13.3 us
    all_gather x1 -> x0, blocking collectives: 10.3 us -> none  [per_device(): lengths_every = lax.all_gather(lengths, ('group', 'dp'), axis=0, tiled=True)]
    ppermute x0 -> x7, starting transfers between devices: none -> 8.65 us  [the longest x3 8.13 us: per_device(): lax.ppermute(all_values, axis_name=('group', 'dp'), perm=[(src_i, (src_i...]
    ppermute x0 -> x7, waiting for transfers between devices: none -> 5.99 us  [the longest x4 5.77 us: per_device(): lax.ppermute(mat_out, axis_name=('group', 'dp'), perm=[(src_i, (src_i + 1...]
    reduce_scatter x1, waiting for transfers between devices: 39.7 us -> 34.1 us  [per_device(): lax.psum_scatter(jnp.dot(attn, w_out, preferred_element_type=jnp.float32)...]
    unnamed x13 -> x12, local copies, waits for them, and re-layouts: 14.1 us -> 14 us
  transfers between devices with their start and end apart: 2 -> 9, of which waited for: 2 -> 8; matrix products, arithmetic and copies ran while one was open for 13% -> 14% of each run, Pallas kernels for 0% -> 0%
where the time goes in v1:
time: 346 us; the launch traced here: 344 us
  matrix products  87.7 us (25%)
  waiting for transfers between devices  86.3 us (25%)
  other arithmetic  70.2 us (20%)
  local copies, waits for them, and re-layouts  69.7 us (20%)
  between operations  14.3 us (4%)
  starting transfers between devices  13.3 us (4%)
    all_to_all x1, waiting for transfers between devices, per_device(): lax.all_to_all(outgoing, ('group', 'dp'), split_axis=1, concat_axis=1, ti...  46.2 us
    reduce_sum x4, other arithmetic, attend(): jnp.sum(expo, axis=-1, keepdims=True)  40.7 us
    dot_general x4, matrix products, attend(): jnp.einsum('kgct,tkd->ckgd', weights, pairs[:, :, 1], preferred_element_t...  36.2 us
    dot_general x4, matrix products, attend(): jnp.einsum('ckgd,tkd->kgct', query_p, pairs[:, :, 0], preferred_element_t...  35.9 us
    reduce_scatter x1, waiting for transfers between devices, per_device(): lax.psum_scatter(jnp.dot(attn, w_out, preferred_element_type=jnp.float32)...  34.1 us
    unnamed x12, local copies, waits for them, and re-layouts  14 us
    select_n x4, other arithmetic, attend(): jnp.where(key_pos < window, (key_pos >= window - history) & (key_pos >= q...  8.15 us
    ppermute x3, starting transfers between devices, per_device(): lax.ppermute(all_values, axis_name=('group', 'dp'), perm=[(src_i, (src_i...  8.13 us
  transfers between devices with their start and end apart: 9, of which 8 were waited for; matrix products, arithmetic and copies ran while one was open for 14% of the time, Pallas kernels for 0%

profile of v1, /device:TPU:0, one launch (start us, length us, event | category | flops | bytes accessed | tf_op | source)
XLA Modules:
  0.0 344.5 jit_solution(14722037447266665043)
XLA Ops:
  27.7 5.3 %convolution_convert_fusion = bf16[1024,512]{1,0:T(8,128)(2,1)S(1)} fusion(bf16[2048,512]{1,0:T(8,128)(2,1)} %param.12, bf16[1024,2048]{1,0:T(8,128)(2,1)} %param.10, f32[2048]{0:T(1024)S(1)} %convert_element_type.40, f32[1024]{0:T(1024)S(1)} %add_rsqrt_fusion), kind=kOutput, calls=%fused_computation.49 | convolution fusion | flops 2156396544 | bytes 7352320 | tf_op jit(solution)/shard_map/dot_general | solution.py:27
  38.1 142.6 %while.14 = (s32[]{:T(128)}, bf16[4,256,512]{2,1,0:T(8,128)(2,1)}, s32[4]{0:T(128)}, bf16[4,2048,1,2,64]{1,4,3,2,0:T(8,128)(2,1)}, bf16[4,256,1,2,64]{1,4,3,2,0:...) while((s32[]{:T(128)}, bf16[4,256,512]{2,1,0:T(8,128)(2,1)}, ...), condition=%wide.region_4.5_spmd.clone.clone, body=%wide.region_1.4_spmd.clone.clone.sunk | while | flops 1268387072 | bytes 63510268 | solution.py:62
  43.3 9.0 %fusion.59 = (f32[8,256]{1,0:T(8,128)S(1)}, f32[2304,256,8]{1,0,2:T(8,128)}) fusion(pred[256,2304]{0,1:T(8,128)(4,1)S(1)} %fusion.58, bf16[4,256,1,8,64]{1,4,3,2,0:T(8,128)(2,1)} %get-tuple-element.301, s32[]{:T(128)S(6)} %copy.58, bf16[256,1,2,64]{0,3,2,1:T(8,128)(2,1)S(1)} %dynamic-slice_bitcast_fusion.4, ...), kind=kOutput, calls=%fused_computation.10.clone.1 | convolution fusion | flops 618723328 | bytes 20324356 | tf_op jit(solution)/shard_map/while/body/eval_jaxpr/ckgd,tkd->kgct/dot_general | solution.py:40
  52.3 10.2 %fusion.60 = f32[8,256]{1,0:T(8,128)S(1)} fusion(f32[2304,256,8]{1,0,2:T(8,128)} %get-tuple-element.275, f32[8,256]{1,0:T(8,128)S(1)} %get-tuple-element.276, pred[256,2304]{0,1:T(8,128)(4,1)S(1)} %fusion.58), kind=kLoop, calls=%fused_computation.9.clone.1 | loop fusion | flops 18872320 | bytes 19480576 | tf_op jit(solution)/shard_map/while/body/eval_jaxpr/reduce_sum | solution.py:53
  62.5 9.0 %fusion.61 = bf16[64,8,256]{2,0,1:T(8,128)(2,1)S(1)} fusion(f32[8,256]{1,0:T(8,128)S(1)} %fusion.60, f32[8,256]{1,0:T(8,128)S(1)} %get-tuple-element.276, f32[2304,256,8]{1,0,2:T(8,128)} %get-tuple-element.275, pred[256,2304]{0,1:T(8,128)(4,1)S(1)} %fusion.58, bf16[2048,1,2,64]{0,3,2,1:T(8,128)(2,1)S(1)} %dynamic-slice_bitcast_fusion.5, ...), kind=kOutput, calls=%fused_computation.17.clone.1 | convolution fusion | flops 628293632 | bytes 20332544 | tf_op jit(solution)/shard_map/while/body/eval_jaxpr/kgct,tkd->ckgd/dot_general | solution.py:54
  78.9 9.0 %fusion.59 = (f32[8,256]{1,0:T(8,128)S(1)}, f32[2304,256,8]{1,0,2:T(8,128)}) fusion(pred[256,2304]{0,1:T(8,128)(4,1)S(1)} %fusion.58, bf16[4,256,1,8,64]{1,4,3,2,0:T(8,128)(2,1)} %get-tuple-element.301, s32[]{:T(128)S(6)} %copy.58, bf16[256,1,2,64]{0,3,2,1:T(8,128)(2,1)S(1)} %dynamic-slice_bitcast_fusion.4, ...), kind=kOutput, calls=%fused_computation.10.clone.1 | convolution fusion | flops 618723328 | bytes 20324356 | tf_op jit(solution)/shard_map/while/body/eval_jaxpr/ckgd,tkd->kgct/dot_general | solution.py:40
  87.9 10.2 %fusion.60 = f32[8,256]{1,0:T(8,128)S(1)} fusion(f32[2304,256,8]{1,0,2:T(8,128)} %get-tuple-element.275, f32[8,256]{1,0:T(8,128)S(1)} %get-tuple-element.276, pred[256,2304]{0,1:T(8,128)(4,1)S(1)} %fusion.58), kind=kLoop, calls=%fused_computation.9.clone.1 | loop fusion | flops 18872320 | bytes 19480576 | tf_op jit(solution)/shard_map/while/body/eval_jaxpr/reduce_sum | solution.py:53
  98.1 9.0 %fusion.61 = bf16[64,8,256]{2,0,1:T(8,128)(2,1)S(1)} fusion(f32[8,256]{1,0:T(8,128)S(1)} %fusion.60, f32[8,256]{1,0:T(8,128)S(1)} %get-tuple-element.276, f32[2304,256,8]{1,0,2:T(8,128)} %get-tuple-element.275, pred[256,2304]{0,1:T(8,128)(4,1)S(1)} %fusion.58, bf16[2048,1,2,64]{0,3,2,1:T(8,128)(2,1)S(1)} %dynamic-slice_bitcast_fusion.5, ...), kind=kOutput, calls=%fused_computation.17.clone.1 | convolution fusion | flops 628293632 | bytes 20332544 | tf_op jit(solution)/shard_map/while/body/eval_jaxpr/kgct,tkd->ckgd/dot_general | solution.py:54
  114.6 9.0 %fusion.59 = (f32[8,256]{1,0:T(8,128)S(1)}, f32[2304,256,8]{1,0,2:T(8,128)}) fusion(pred[256,2304]{0,1:T(8,128)(4,1)S(1)} %fusion.58, bf16[4,256,1,8,64]{1,4,3,2,0:T(8,128)(2,1)} %get-tuple-element.301, s32[]{:T(128)S(6)} %copy.58, bf16[256,1,2,64]{0,3,2,1:T(8,128)(2,1)S(1)} %dynamic-slice_bitcast_fusion.4, ...), kind=kOutput, calls=%fused_computation.10.clone.1 | convolution fusion | flops 618723328 | bytes 20324356 | tf_op jit(solution)/shard_map/while/body/eval_jaxpr/ckgd,tkd->kgct/dot_general | solution.py:40
  123.6 10.2 %fusion.60 = f32[8,256]{1,0:T(8,128)S(1)} fusion(f32[2304,256,8]{1,0,2:T(8,128)} %get-tuple-element.275, f32[8,256]{1,0:T(8,128)S(1)} %get-tuple-element.276, pred[256,2304]{0,1:T(8,128)(4,1)S(1)} %fusion.58), kind=kLoop, calls=%fused_computation.9.clone.1 | loop fusion | flops 18872320 | bytes 19480576 | tf_op jit(solution)/shard_map/while/body/eval_jaxpr/reduce_sum | solution.py:53
  133.8 9.0 %fusion.61 = bf16[64,8,256]{2,0,1:T(8,128)(2,1)S(1)} fusion(f32[8,256]{1,0:T(8,128)S(1)} %fusion.60, f32[8,256]{1,0:T(8,128)S(1)} %get-tuple-element.276, f32[2304,256,8]{1,0,2:T(8,128)} %get-tuple-element.275, pred[256,2304]{0,1:T(8,128)(4,1)S(1)} %fusion.58, bf16[2048,1,2,64]{0,3,2,1:T(8,128)(2,1)S(1)} %dynamic-slice_bitcast_fusion.5, ...), kind=kOutput, calls=%fused_computation.17.clone.1 | convolution fusion | flops 628293632 | bytes 20332544 | tf_op jit(solution)/shard_map/while/body/eval_jaxpr/kgct,tkd->ckgd/dot_general | solution.py:54
  150.2 9.0 %fusion.59 = (f32[8,256]{1,0:T(8,128)S(1)}, f32[2304,256,8]{1,0,2:T(8,128)}) fusion(pred[256,2304]{0,1:T(8,128)(4,1)S(1)} %fusion.58, bf16[4,256,1,8,64]{1,4,3,2,0:T(8,128)(2,1)} %get-tuple-element.301, s32[]{:T(128)S(6)} %copy.58, bf16[256,1,2,64]{0,3,2,1:T(8,128)(2,1)S(1)} %dynamic-slice_bitcast_fusion.4, ...), kind=kOutput, calls=%fused_computation.10.clone.1 | convolution fusion | flops 618723328 | bytes 20324356 | tf_op jit(solution)/shard_map/while/body/eval_jaxpr/ckgd,tkd->kgct/dot_general | solution.py:40
  159.2 10.2 %fusion.60 = f32[8,256]{1,0:T(8,128)S(1)} fusion(f32[2304,256,8]{1,0,2:T(8,128)} %get-tuple-element.275, f32[8,256]{1,0:T(8,128)S(1)} %get-tuple-element.276, pred[256,2304]{0,1:T(8,128)(4,1)S(1)} %fusion.58), kind=kLoop, calls=%fused_computation.9.clone.1 | loop fusion | flops 18872320 | bytes 19480576 | tf_op jit(solution)/shard_map/while/body/eval_jaxpr/reduce_sum | solution.py:53
  169.4 9.0 %fusion.61 = bf16[64,8,256]{2,0,1:T(8,128)(2,1)S(1)} fusion(f32[8,256]{1,0:T(8,128)S(1)} %fusion.60, f32[8,256]{1,0:T(8,128)S(1)} %get-tuple-element.276, f32[2304,256,8]{1,0,2:T(8,128)} %get-tuple-element.275, pred[256,2304]{0,1:T(8,128)(4,1)S(1)} %fusion.58, bf16[2048,1,2,64]{0,3,2,1:T(8,128)(2,1)S(1)} %dynamic-slice_bitcast_fusion.5, ...), kind=kOutput, calls=%fused_computation.17.clone.1 | convolution fusion | flops 628293632 | bytes 20332544 | tf_op jit(solution)/shard_map/while/body/eval_jaxpr/kgct,tkd->ckgd/dot_general | solution.py:54
  180.8 6.8 %fusion.45 = f32[1024,2048]{1,0:T(8,128)} fusion(bf16[1024,512]{1,0:T(8,128)(2,1)} %bitcast.98, bf16[512,2048]{1,0:T(8,128)(2,1)S(1)} %copy-done), kind=kOutput, calls=%fused_computation.92 | convolution fusion | flops 2147483648 | bytes 11534336 | tf_op jit(solution)/shard_map/dot_general | solution.py:65
  205.6 6.5 %gather_fusion = bf16[32,4,128,128]{3,2,1,0:T(8,128)(2,1)} fusion(bf16[4,64,128,128]{3,2,1,0:T(8,128)(2,1)} %bitcast.96, s32[1024]{0:T(1024)S(1)} %pad_clamp_fusion.1), kind=kCustom, calls=%fused_computation | custom fusion | bytes 8388736 | tf_op jit(solution)/shard_map/jit(_take)/gather | solution.py:127
  212.1 4.7 %select_bitcast_fusion.1 = bf16[4,32,128,128]{3,2,0,1:T(8,128)(2,1)} fusion(bf16[32,4,128,128]{3,2,1,0:T(8,128)(2,1)} %gather_fusion, pred[32]{0:T(512)(128)(4,1)S(1)} %compare_and_fusion), kind=kLoop, calls=%fused_computation.48 | loop fusion | flops 2097152 | bytes 8388640 | tf_op jit(solution)/shard_map/jit(_take)/select_n | solution.py:127
  216.8 4.6 %all-to-all-start = ((bf16[4,32,128,128]{3,2,0,1:T(8,128)(2,1)}), bf16[4,32,128,128]{3,2,0,1:T(8,128)(2,1)}, u32[]{:S(2)}, u32[]{:S(2)}) async-start(bf16[4,32,128,128]{3,2,0,1:T(8,128)(2,1)} %select_bitcast_fusion.1), calls=%async_computation.1 | async-start | bytes 8388608 | tf_op jit(solution)/shard_map/all_to_all | solution.py:128
  224.3 46.2 %all-to-all-done = bf16[4,32,128,128]{3,2,0,1:T(8,128)(2,1)} async-done(((bf16[4,32,128,128]{3,2,0,1:T(8,128)(2,1)}), bf16[4,32,128,128]{3,2,0,1:T(8,128)(2,1)}, u32[]{:S(2)}, u32[]{:S(2)}) %all-to-all-start) | async-done | bytes 4194336 | tf_op jit(solution)/shard_map/all_to_all | solution.py:128
  270.5 4.7 %copy.44 = bf16[4,32,128,128]{3,2,1,0:T(8,128)(2,1)} copy(bf16[4,32,128,128]{3,2,0,1:T(8,128)(2,1)} %all-to-all-done) | data formatting | bytes 8388608 | tf_op jit(solution)/shard_map/all_to_all | solution.py:128
  275.2 7.8 %gather_fusion.1 = bf16[64,4,128,128]{3,2,1,0:T(8,128)(2,1)} fusion(bf16[4,32,128,128]{3,2,1,0:T(8,128)(2,1)} %copy.44, s32[1024]{0:T(1024)S(1)} %pad_clamp_fusion), kind=kCustom, calls=%fused_computation.1 | custom fusion | bytes 16777472 | tf_op jit(solution)/shard_map/jit(_take)/gather | solution.py:137
  283.0 7.3 %select_bitcast_fusion = bf16[4,64,128,128]{3,2,0,1:T(8,128)(2,1)} fusion(bf16[64,4,128,128]{3,2,1,0:T(8,128)(2,1)} %gather_fusion.1, pred[64]{0:T(512)(128)(4,1)S(1)} %compare_and_fusion.1), kind=kLoop, calls=%fused_computation.47 | loop fusion | flops 4194304 | bytes 16777280 | tf_op jit(solution)/shard_map/jit(_take)/select_n | solution.py:137
  290.3 10.5 %copy.45 = bf16[4,64,128,128]{3,2,1,0:T(8,128)(2,1)} copy(bf16[4,64,128,128]{3,2,0,1:T(8,128)(2,1)} %select_bitcast_fusion) | data formatting | bytes 16777216
  300.9 34.1 %reduce-scatter.2.cloned.1.call-done = f32[256,2048]{1,0:T(8,128)} async-done(((f32[1024,2048]{1,0:T(8,128)}), f32[256,2048]{1,0:T(8,128)}) %reduce-scatter.2.cloned.1.call-update) | async-done | bytes 2097168 | tf_op jit(solution)/shard_map/reduce_scatter | solution.py:64
  (134 shorter events, 75.9 us)
Async XLA Ops:
  7.2 173.6 %copy-start = (bf16[512,2048]{1,0:T(8,128)(2,1)S(1)}, bf16[512,2048]{1,0:T(8,128)(2,1)}, u32[]{:S(2)}) copy-start(bf16[512,2048]{1,0:T(8,128)(2,1)} %param.14) | copy-start | bytes 6291460
  7.2 13.2 %copy-start.2 = (bf16[2048]{0:T(1024)(128)(2,1)S(1)}, bf16[2048]{0:T(1024)(128)(2,1)}, u32[]{:S(2)}) copy-start(bf16[2048]{0:T(1024)(128)(2,1)} %param.11) | copy-start | bytes 12292
  7.2 327.7 %reduce-scatter.2.cloned.1.call-start = ((), (), s32[]{:S(2)}) async-start(), calls=%async_computation.2 | async-start | bytes 10485760 | tf_op jit(solution)/shard_map/reduce_scatter | solution.py:64
  62.4 9.1 %copy-start.4 = (s32[4]{0:T(128)S(1)}, s32[4]{0:T(128)}, u32[]{:S(2)}) copy-start(s32[4]{0:T(128)} %get-tuple-element.297) | copy-start | bytes 52 | tf_op jit(solution)/shard_map/while
  98.1 9.1 %copy-start.4 = (s32[4]{0:T(128)S(1)}, s32[4]{0:T(128)}, u32[]{:S(2)}) copy-start(s32[4]{0:T(128)} %get-tuple-element.297) | copy-start | bytes 52 | tf_op jit(solution)/shard_map/while
  133.8 9.1 %copy-start.4 = (s32[4]{0:T(128)S(1)}, s32[4]{0:T(128)}, u32[]{:S(2)}) copy-start(s32[4]{0:T(128)} %get-tuple-element.297) | copy-start | bytes 52 | tf_op jit(solution)/shard_map/while
  169.4 9.1 %copy-start.4 = (s32[4]{0:T(128)S(1)}, s32[4]{0:T(128)}, u32[]{:S(2)}) copy-start(s32[4]{0:T(128)} %get-tuple-element.297) | copy-start | bytes 52 | tf_op jit(solution)/shard_map/while
  180.8 6.8 %copy-start.3 = (s32[4,2]{0,1:T(2,128)S(1)}, s32[4,2]{0,1:T(2,128)}, u32[]{:S(2)}) copy-start(s32[4,2]{0,1:T(2,128)} %param.16) | copy-start | bytes 100
  180.8 10.3 %copy-start.1 = (s32[32,16]{0,1:T(8,128)S(1)}, s32[32,16]{0,1:T(8,128)}, u32[]{:S(2)}) copy-start(s32[32,16]{0,1:T(8,128)} %param.17) | copy-start | bytes 6148
  187.6 4.6 %collective-permute-start = (s32[4,2]{0,1:T(2,128)S(1)}, s32[4,2]{0,1:T(2,128)S(1)}, u32[]{:S(2)}, u32[]{:S(2)}) collective-permute-start(s32[4,2]{0,1:T(2,128)S(1)} %copy-done.3), channel_id=1, source_target_pairs={{0,4},{4,8},{8,12},{12,16},{16,20},{20,24},{24,28},{28,0},{1,5},{5... | collective-permute-start | bytes 104 | tf_op jit(solution)/shard_map/ppermute | solution.py:97
  188.1 4.2 %collective-permute-start.1 = (s32[4,2]{0,1:T(2,128)S(1)}, s32[4,2]{0,1:T(2,128)S(1)}, u32[]{:S(2)}, u32[]{:S(2)}) collective-permute-start(s32[4,2]{0,1:T(2,128)S(1)} %copy-done.3), channel_id=1, source_target_pairs={{0,28},{4,0},{8,4},{12,8},{16,12},{20,16},{24,20},{28,24},{1,29},{... | collective-permute-start | bytes 104 | tf_op jit(solution)/shard_map/ppermute | solution.py:106
  192.3 3.9 %collective-permute-start.2 = (s32[4,2]{0,1:T(2,128)S(1)}, s32[4,2]{0,1:T(2,128)S(1)}, u32[]{:S(2)}, u32[]{:S(2)}) collective-permute-start(s32[4,2]{0,1:T(2,128)S(1)} %collective-permute-done), channel_id=1, source_target_pairs={{0,4},{4,8},{8,12},{12,16},{16,20},{20,24},{24,28},{28,0},{1,5},{5... | collective-permute-start | bytes 104 | tf_op jit(solution)/shard_map/ppermute | solution.py:97
  192.4 3.9 %collective-permute-start.3 = (s32[4,2]{0,1:T(2,128)S(1)}, s32[4,2]{0,1:T(2,128)S(1)}, u32[]{:S(2)}, u32[]{:S(2)}) collective-permute-start(s32[4,2]{0,1:T(2,128)S(1)} %collective-permute-done.1), channel_id=1, source_target_pairs={{0,28},{4,0},{8,4},{12,8},{16,12},{20,16},{24,20},{28,24},{1,29},{... | collective-permute-start | bytes 104 | tf_op jit(solution)/shard_map/ppermute | solution.py:106
  196.2 3.9 %collective-permute-start.4 = (s32[4,2]{0,1:T(2,128)S(1)}, s32[4,2]{0,1:T(2,128)S(1)}, u32[]{:S(2)}, u32[]{:S(2)}) collective-permute-start(s32[4,2]{0,1:T(2,128)S(1)} %collective-permute-done.2), channel_id=1, source_target_pairs={{0,4},{4,8},{8,12},{12,16},{16,20},{20,24},{24,28},{28,0},{1,5},{5... | collective-permute-start | bytes 104 | tf_op jit(solution)/shard_map/ppermute | solution.py:97
  196.3 4.0 %collective-permute-start.5 = (s32[4,2]{0,1:T(2,128)S(1)}, s32[4,2]{0,1:T(2,128)S(1)}, u32[]{:S(2)}, u32[]{:S(2)}) collective-permute-start(s32[4,2]{0,1:T(2,128)S(1)} %collective-permute-done.3), channel_id=1, source_target_pairs={{0,28},{4,0},{8,4},{12,8},{16,12},{20,16},{24,20},{28,24},{1,29},{... | collective-permute-start | bytes 104 | tf_op jit(solution)/shard_map/ppermute | solution.py:106
  200.0 3.9 %collective-permute-start.6 = (s32[4,2]{0,1:T(2,128)S(1)}, s32[4,2]{0,1:T(2,128)S(1)}, u32[]{:S(2)}, u32[]{:S(2)}) collective-permute-start(s32[4,2]{0,1:T(2,128)S(1)} %collective-permute-done.4), channel_id=1, source_target_pairs={{0,4},{4,8},{8,12},{12,16},{16,20},{20,24},{24,28},{28,0},{1,5},{5... | collective-permute-start | bytes 104 | tf_op jit(solution)/shard_map/ppermute | solution.py:97
  216.8 53.7 %all-to-all-start = ((bf16[4,32,128,128]{3,2,0,1:T(8,128)(2,1)}), bf16[4,32,128,128]{3,2,0,1:T(8,128)(2,1)}, u32[]{:S(2)}, u32[]{:S(2)}) async-start(bf16[4,32,128,128]{3,2,0,1:T(8,128)(2,1)} %select_bitcast_fusion.1), calls=%async_computation.1 | async-start | bytes 8388608 | tf_op jit(solution)/shard_map/all_to_all | solution.py:128
Sparse Core Ops, SparseCore 0:
  187.7 147.1 reduce-scatter.1
